TPU v7x, 512 devices: a whole 4x4x16 slice. The times are simulated.
512 devices in a mesh: tm: 8 (over y, core), chan: 64 (over z, x).
Axes of the slice: x: 4, y: 4, z: 16, core: 2. Of those that a mesh axis runs over, the one named last changes fastest.
Arguments:
- spectra: bfloat16 [8, 8192, 8192], P('tm', 'chan'), may hold values from -6 to 6
- block_counts: int32 [64], replicated, may hold values from 1 to 128, 6144 in all
- pairs: int32 [96, 3], replicated, may hold values from 0 to 63, as said below
Outputs:
- stacks: float32 [192, 128, 1024], P('chan', 'tm')
Inputs may be any that keep to these rules, and one draw needn't show every extreme that they name: `pairs`: each owner holds at most 3 pair blocks and some owner holds exactly 3; all pair blocks of one owner share their source block; a target block never equals its source block.
All inputs are finite; a program needn't handle non-finite values.
Results may differ from a plain program's by a relative error of at most 0.0049.
Values may be sent and summed in bfloat16 or wider, within the bound.
A program may use at most 128 MiB of HBM per device.

v0:
```python
import math
import jax
import jax.numpy as jnp
from jax import lax
from jax.sharding import PartitionSpec as P

F = 4096
BAND = 64
LAGS = 8
SLOTS = 3


def phase_tables():
    freq_index = (
        jnp.arange(F // BAND, dtype=jnp.int32)[:, None] * BAND
        + jnp.arange(BAND, dtype=jnp.int32)[None, :]
    )
    lag_values = jnp.arange(LAGS, dtype=jnp.int32) - LAGS // 2
    phase = jnp.mod(lag_values[:, None, None] * freq_index[None], 2 * F)
    angle = jnp.pi * phase.astype(jnp.float32) / F
    return (jnp.cos(angle), jnp.sin(angle))


def whiten(raw, live_count):
    segs, rows, width = raw.shape
    values = raw.astype(jnp.float32).reshape(segs, rows, width // (2 * BAND), 2, BAND)
    power = jnp.mean(values[..., 0, :] ** 2 + values[..., 1, :] ** 2, axis=-1)
    alive = (jnp.arange(rows, dtype=jnp.int32) < live_count).astype(jnp.float32)
    scaled = values * lax.rsqrt(power + 1e-06)[..., None, None] * alive[None, :, None, None, None]
    return scaled.astype(jnp.bfloat16).reshape(segs, rows, width)


def correlate(source, target, cosine, sine, scale):
    groups, segs, rows, width = source.shape
    bands = width // (2 * BAND)
    src = source.reshape(groups, segs, rows, bands, 2, BAND)
    tgt = (
        target.reshape(groups, segs, rows, bands, 2, BAND)
        .transpose(1, 2, 0, 3, 4, 5)
        .astype(jnp.float32)
    )
    real_part = tgt[..., 0, :][:, None]
    imag_part = tgt[..., 1, :][:, None]
    cos_b = cosine.reshape(LAGS, groups, bands, BAND)[None, :, None]
    sin_b = sine.reshape(LAGS, groups, bands, BAND)[None, :, None]
    mod_real = real_part * cos_b + imag_part * sin_b
    mod_imag = imag_part * cos_b - real_part * sin_b
    moved = jnp.stack([mod_real, mod_imag], axis=-2).astype(jnp.bfloat16)
    corr = jnp.einsum("ksiqpf,smjkqpf->imj", src, moved, preferred_element_type=jnp.float32)
    return (corr * scale).reshape(rows, LAGS * rows)


def per_device(spectra, block_counts, pairs):
    chan_count = lax.axis_size("chan")
    my_index = lax.axis_index("chan")
    segs, rows, width = spectra.shape
    scale = 1.0 / math.sqrt(2.0 * F * segs * lax.axis_size("tm"))
    cosine, sine = phase_tables()
    device_ids = jnp.arange(chan_count, dtype=jnp.int32)
    live_count = jnp.sum(jnp.where(device_ids == my_index, block_counts, 0))
    whitened = whiten(spectra, live_count)
    held = lax.all_to_all(whitened[None], "chan", split_axis=3, concat_axis=0, tiled=True)
    owners = pairs[:, 2]
    places = jnp.arange(pairs.shape[0], dtype=jnp.int32)
    earlier = (owners[:, None] == owners[None, :]) & (places[None, :] < places[:, None])
    ranks = jnp.sum(earlier.astype(jnp.int32), axis=1)
    slot_ids = jnp.arange(SLOTS, dtype=jnp.int32)
    matches = (
        (owners[None, None, :] == device_ids[:, None, None])
        & (ranks[None, None, :] == slot_ids[None, :, None])
    ).astype(jnp.int32)
    source_table = jnp.sum(matches * pairs[:, 0][None, None, :], axis=2)
    target_table = jnp.sum(matches * pairs[:, 1][None, None, :], axis=2)
    valid_table = jnp.sum(matches, axis=2)
    my_valid = jnp.sum(jnp.where(device_ids[:, None] == my_index, valid_table, 0), axis=0).astype(
        jnp.float32
    )
    send_source = jnp.take(held, source_table, axis=0)
    send_target = jnp.take(held, target_table, axis=0)
    src_all = lax.all_to_all(send_source, "chan", split_axis=0, concat_axis=0, tiled=True)
    tgt_all = lax.all_to_all(send_target, "chan", split_axis=0, concat_axis=0, tiled=True)

    def one_item(position):
        src_one = lax.dynamic_index_in_dim(src_all, position, 1, False)
        tgt_one = lax.dynamic_index_in_dim(tgt_all, position, 1, False)
        return correlate(src_one, tgt_one, cosine, sine, scale)

    results = lax.map(one_item, jnp.arange(src_all.shape[1], dtype=jnp.int32))
    results = results * my_valid[:, None, None]
    return lax.psum_scatter(results, "tm", scatter_dimension=1, tiled=True)


def solution(mesh):
    placed = (P("tm", "chan", None), P(), P())
    return jax.shard_map(
        per_device, mesh=mesh, in_specs=placed, out_specs=P("chan", "tm", None), check_vma=False
    )
```

profile of v0, /device:TPU:2, one launch (start us, length us, event | category | flops | bytes accessed | tf_op | source)
XLA Modules:
  0.0 956.7 jit_solution(11877595196581559371)
XLA Ops:
  6.5 3.2 copy.33
  10.3 0.6 fusion.23
  10.9 0.6 select_reduce_fusion.1
  11.5 0.6 compare_convert_fusion
  12.8 33.3 %copy.53 = bf16[1,1,128,8192]{2,1,0,3:T(2,128)(2,1)} copy(bf16[1,1,128,8192]{2,3,1,0:T(8,128)(2,1)S(1)} %fusion.21) | data formatting | bytes 4194304 | tf_op jit(solution)/shard_map/convert_element_type | solution.py:30
  46.5 45.2 %reduce.2 = bf16[8192,128]{1,0:T(8,128)(2,1)S(1)} reduce(bf16[8192,1,1,128]{3,2,1,0:T(2,128)(2,1)} %bitcast.78, bf16[]{:T(256)} %broadcast.250), dimensions={1,2}, to_apply=%bitcast.55.reduce_sub_computation | reduce | bytes 4194306
  91.7 2.1 reshape.305
  93.8 18.8 %all-to-all-start = ((bf16[64,2,8192]{2,1,0:T(2,128)(2,1)}), bf16[64,2,8192]{2,1,0:T(2,128)(2,1)S(1)}, u32[]{:S(2)}, u32[]{:S(2)}) async-start(bf16[64,2,8192]{2,1,0:T(2,128)(2,1)} %reshape.305), calls=%async_computation | async-start | bytes 4194304 | tf_op jit(solution)/shard_map/all_to_all | solution.py:62
  113.5 99.2 %all-to-all-done = bf16[64,2,8192]{2,1,0:T(2,128)(2,1)S(1)} async-done(((bf16[64,2,8192]{2,1,0:T(2,128)(2,1)}), bf16[64,2,8192]{2,1,0:T(2,128)(2,1)S(1)}, u32[]{:S(2)}, u32[]{:S(2)}) %all-to-all-start) | async-done | bytes 2097184 | tf_op jit(solution)/shard_map/all_to_all | solution.py:62
  212.8 6.8 reshape.306
  219.5 3.8 copy.50
  223.3 3.2 copy.35
  226.5 8.0 gather_fusion
  234.5 8.6 copy.37
  243.2 6.1 broadcast_select_fusion
  249.3 6.1 all-to-all-start.1
  255.7 7.9 gather_fusion.1
  263.7 6.0 select_bitcast_fusion
  269.7 265.0 %all-to-all-done.1 = bf16[64,3,1,128,128]{3,4,2,1,0:T(8,128)(2,1)} async-done(((bf16[64,3,1,128,128]{3,4,2,1,0:T(8,128)(2,1)}), bf16[64,3,1,128,128]{3,4,2,1,0:T(8,128)(2,1)}, u32[]{:S(2)}, u32[]{:S(2)}) %all-to-all-start.1) | async-done | bytes 6291488 | tf_op jit(solution)/shard_map/all_to_all | solution.py:80
  534.7 6.1 all-to-all-start.2
  541.3 0.7 iota_add_fusion
  542.0 278.2 %all-to-all-done.2 = bf16[64,3,1,128,128]{4,3,1,2,0:T(8,128)(2,1)} async-done(((bf16[64,3,1,128,128]{4,3,1,2,0:T(8,128)(2,1)}), bf16[64,3,1,128,128]{4,3,1,2,0:T(8,128)(2,1)}, u32[]{:S(2)}, u32[]{:S(2)}) %all-to-all-start.2) | async-done | bytes 6291488 | tf_op jit(solution)/shard_map/all_to_all | solution.py:81
  820.2 94.2 %while.13 = (s32[]{:T(128)}, f32[3,128,1024]{2,1,0:T(8,128)}, s32[3]{0:T(128)S(1)}, bf16[64,3,1,128,128]{3,4,2,1,0:T(8,128)(2,1)}, bf16[64,3,1,128,128]{4,3,1,2,...) while((s32[]{:T(128)}, f32[3,128,1024]{2,1,0:T(8,128)}, ...), condition=%wide.region_6.8_spmd.clone.clone.clone, body=%wide.region_5.7_spmd.clone.clone.clone.sunk | while | flops 2216230912 | bytes 70271672 | solution.py:88
  820.2 0.6 dynamic_slice.27
  822.6 3.2 constant_dynamic-slice_fusion.5
  825.8 3.2 copy.56
  829.9 1.9 fusion.35
  831.7 9.9 %add_convert_fusion.2 = (bf16[8,128,64,1,64]{1,4,3,0,2:T(8,128)(2,1)S(1)}, bf16[8,128,64,1,64]{1,4,3,0,2:T(8,128)(2,1)S(1)}) fusion(f32[8,64,64]{2,0,1:T(8,128)S(1)} %get-tuple-element.231, f32[128,64,64]{0,2,1:T(8,128)S(1)} %get-tuple-element.232, f32[8,64,64]{2,0,1:T(8,128)S(1)} %get-tuple-element.233, f32[128,64,64]{0,2,1:T(8,128)S(1)} %get-tuple-element.234), kind=kLoop, calls=%fused_computation.9.clone.1 | loop fusion | flops 33554432 | bytes 21233664 | tf_op jit(solution)/shard_map/convert.2
  841.6 1.7 constant_dynamic-slice_fusion.4
  843.4 7.1 fusion.36
  850.7 0.8 constant_dynamic-update-slice_fusion.2
  851.6 0.6 dynamic_slice.27
  854.0 3.2 constant_dynamic-slice_fusion.5
  857.2 3.2 copy.56
  861.3 1.9 fusion.35
  863.1 9.9 %add_convert_fusion.2 = (bf16[8,128,64,1,64]{1,4,3,0,2:T(8,128)(2,1)S(1)}, bf16[8,128,64,1,64]{1,4,3,0,2:T(8,128)(2,1)S(1)}) fusion(f32[8,64,64]{2,0,1:T(8,128)S(1)} %get-tuple-element.231, f32[128,64,64]{0,2,1:T(8,128)S(1)} %get-tuple-element.232, f32[8,64,64]{2,0,1:T(8,128)S(1)} %get-tuple-element.233, f32[128,64,64]{0,2,1:T(8,128)S(1)} %get-tuple-element.234), kind=kLoop, calls=%fused_computation.9.clone.1 | loop fusion | flops 33554432 | bytes 21233664 | tf_op jit(solution)/shard_map/convert.2
  873.1 1.7 constant_dynamic-slice_fusion.4
  874.8 7.1 fusion.36
  882.2 0.9 constant_dynamic-update-slice_fusion.2
  885.4 3.2 constant_dynamic-slice_fusion.5
  888.7 3.2 copy.56
  892.7 1.9 fusion.35
  894.6 9.9 %add_convert_fusion.2 = (bf16[8,128,64,1,64]{1,4,3,0,2:T(8,128)(2,1)S(1)}, bf16[8,128,64,1,64]{1,4,3,0,2:T(8,128)(2,1)S(1)}) fusion(f32[8,64,64]{2,0,1:T(8,128)S(1)} %get-tuple-element.231, f32[128,64,64]{0,2,1:T(8,128)S(1)} %get-tuple-element.232, f32[8,64,64]{2,0,1:T(8,128)S(1)} %get-tuple-element.233, f32[128,64,64]{0,2,1:T(8,128)S(1)} %get-tuple-element.234), kind=kLoop, calls=%fused_computation.9.clone.1 | loop fusion | flops 33554432 | bytes 21233664 | tf_op jit(solution)/shard_map/convert.2
  904.5 1.7 constant_dynamic-slice_fusion.4
  906.2 7.1 fusion.36
  913.6 0.8 constant_dynamic-update-slice_fusion.2
  914.4 2.9 broadcast_multiply_fusion
  917.3 32.6 %reduce-scatter.2.cloned.1.call-done = f32[3,16,1024]{2,1,0:T(8,128)} async-done(((f32[3,128,1024]{2,1,0:T(8,128)}), f32[3,16,1024]{2,1,0:T(8,128)}) %reduce-scatter.2.cloned.1.call-update) | async-done | bytes 196624 | tf_op jit(solution)/shard_map/reduce_scatter | solution.py:90
  (42 shorter events, 6.8 us)
Async XLA Ops:
  9.8 1.1 copy-start.1
  91.7 20.9 %copy-start = (s32[96,3]{0,1:T(4,128)S(1)}, s32[96,3]{0,1:T(4,128)}, u32[]{:S(2)}) copy-start(s32[96,3]{0,1:T(4,128)} %param.9) | copy-start | bytes 3460
  93.8 118.9 %all-to-all-start = ((bf16[64,2,8192]{2,1,0:T(2,128)(2,1)}), bf16[64,2,8192]{2,1,0:T(2,128)(2,1)S(1)}, u32[]{:S(2)}, u32[]{:S(2)}) async-start(bf16[64,2,8192]{2,1,0:T(2,128)(2,1)} %reshape.305), calls=%async_computation | async-start | bytes 4194304 | tf_op jit(solution)/shard_map/all_to_all | solution.py:62
  249.3 285.5 %all-to-all-start.1 = ((bf16[64,3,1,128,128]{3,4,2,1,0:T(8,128)(2,1)}), bf16[64,3,1,128,128]{3,4,2,1,0:T(8,128)(2,1)}, u32[]{:S(2)}, u32[]{:S(2)}) async-start(bf16[64,3,1,128,128]{3,4,2,1,0:T(8,128)(2,1)} %broadcast_select_fusion), calls=%async_computation.1 | async-start | bytes 12582912 | tf_op jit(solution)/shard_map/all_to_all | solution.py:80
  534.7 285.4 %all-to-all-start.2 = ((bf16[64,3,1,128,128]{4,3,1,2,0:T(8,128)(2,1)}), bf16[64,3,1,128,128]{4,3,1,2,0:T(8,128)(2,1)}, u32[]{:S(2)}, u32[]{:S(2)}) async-start(bf16[64,3,1,128,128]{4,3,1,2,0:T(8,128)(2,1)} %select_bitcast_fusion), calls=%async_computation.2 | async-start | bytes 12582912 | tf_op jit(solution)/shard_map/all_to_all | solution.py:81
  540.8 409.1 %reduce-scatter.2.cloned.1.call-start = ((), (), s32[]{:S(2)}) async-start(), calls=%async_computation.4 | async-start | bytes 1769472 | tf_op jit(solution)/shard_map/reduce_scatter | solution.py:90
Sparse Core Ops, SparseCore 0:
  917.4 32.4 reduce-scatter.1
where the time goes:
time: 958 us; the launch traced here: 957 us
  waiting for transfers between devices  675 us (70%)
  local copies, waits for them, and re-layouts  109 us (11%)
  other arithmetic  101 us (11%)
  starting transfers between devices  31.3 us (3%)
  matrix products  21.4 us (2%)
  between operations  13.6 us (1%)
    all_to_all x1, waiting for transfers between devices, per_device(): lax.all_to_all(send_target, 'chan', split_axis=0, concat_axis=0, tiled=True)  278 us
    all_to_all x1, waiting for transfers between devices, per_device(): lax.all_to_all(send_source, 'chan', split_axis=0, concat_axis=0, tiled=True)  265 us
    all_to_all x1, waiting for transfers between devices, per_device(): lax.all_to_all(whitened[None], 'chan', split_axis=3, concat_axis=0, tiled...  99.2 us
    unnamed x1, other arithmetic  45.2 us
    convert_element_type x1, local copies, waits for them, and re-layouts, whiten(): return scaled.astype(jnp.bfloat16).reshape(segs, rows, width)  33.3 us
    reduce_scatter x1, waiting for transfers between devices, per_device(): return lax.psum_scatter(results, 'tm', scatter_dimension=1, tiled=True)  32.6 us
    another operation x3, other arithmetic  29.7 us
    dot_general x3, matrix products, correlate(): jnp.einsum('ksiqpf,smjkqpf->imj', src, moved, preferred_element_type=jnp....  21.4 us
  transfers between devices with their start and end apart: 4, of which 4 were waited for; matrix products, arithmetic and copies ran while one was open for 2% of the time, Pallas kernels for 0%

commit v1 on v0

--- a/solution.py
+++ b/solution.py
@@ -59,7 +59,12 @@
     device_ids = jnp.arange(chan_count, dtype=jnp.int32)
     live_count = jnp.sum(jnp.where(device_ids == my_index, block_counts, 0))
     whitened = whiten(spectra, live_count)
-    held = lax.all_to_all(whitened[None], "chan", split_axis=3, concat_axis=0, tiled=True)
+    held = jnp.concatenate(
+        lax.all_to_all(
+            jnp.stack(jnp.split(whitened[None], lax.axis_size("chan"), axis=3)), "chan", 0, 0
+        ),
+        axis=0,
+    )
     owners = pairs[:, 2]
     places = jnp.arange(pairs.shape[0], dtype=jnp.int32)
     earlier = (owners[:, None] == owners[None, :]) & (places[None, :] < places[:, None])

time: 958 us -> 900 us (0.939)
  other arithmetic: 101 us -> 53.1 us
  local copies, waits for them, and re-layouts: 109 us -> 97.7 us
    unnamed x1 -> x0, other arithmetic: 45.2 us -> none
    convert_element_type x1 -> x0, local copies, waits for them, and re-layouts: 33.3 us -> none  [whiten(): return scaled.astype(jnp.bfloat16).reshape(segs, rows, width)]
    unnamed x9 -> x68, local copies, waits for them, and re-layouts: 16.4 us -> 41.3 us
    all_to_all x1, waiting for transfers between devices: 265 us -> 279 us  [per_device(): lax.all_to_all(send_source, 'chan', split_axis=0, concat_axis=0, tiled=True)]
    all_to_all x1, waiting for transfers between devices: 278 us -> 265 us  [per_device(): lax.all_to_all(send_target, 'chan', split_axis=0, concat_axis=0, tiled=True)]
where the time goes in v1:
time: 900 us; the launch traced here: 898 us
  waiting for transfers between devices  676 us (75%)
  local copies, waits for them, and re-layouts  97.7 us (11%)
  other arithmetic  53.1 us (6%)
  starting transfers between devices  31 us (3%)
  matrix products  21.4 us (2%)
  between operations  13.6 us (2%)
    all_to_all x1, waiting for transfers between devices, per_device(): lax.all_to_all(send_source, 'chan', split_axis=0, concat_axis=0, tiled=True)  279 us
    all_to_all x1, waiting for transfers between devices, per_device(): lax.all_to_all(send_target, 'chan', split_axis=0, concat_axis=0, tiled=True)  265 us
    all_to_all x1, waiting for transfers between devices, per_device(): lax.all_to_all(jnp.stack(jnp.split(whitened[None], lax.axis_size('chan'),...  99.2 us
    unnamed x68, local copies, waits for them, and re-layouts  41.3 us
    reduce_scatter x1, waiting for transfers between devices, per_device(): return lax.psum_scatter(results, 'tm', scatter_dimension=1, tiled=True)  32.6 us
    another operation x3, other arithmetic  29.7 us
    dot_general x3, matrix products, correlate(): jnp.einsum('ksiqpf,smjkqpf->imj', src, moved, preferred_element_type=jnp....  21.4 us
    dynamic_slice x6, local copies, waits for them, and re-layouts, one_item(): tgt_one = lax.dynamic_index_in_dim(tgt_all, position, 1, False)  19.3 us
  transfers between devices with their start and end apart: 4, of which 4 were waited for; matrix products, arithmetic and copies ran while one was open for 2% of the time, Pallas kernels for 0%

profile of v1, /device:TPU:2, one launch (start us, length us, event | category | flops | bytes accessed | tf_op | source)
XLA Modules:
  0.0 898.4 jit_solution(15878176134808692359)
XLA Ops:
  6.5 3.2 copy.28
  10.3 0.6 fusion.23
  10.9 0.6 select_reduce_fusion.1
  11.5 0.6 compare_convert_fusion
  15.8 0.6 constant_dynamic-update-slice_fusion.59
  18.8 0.6 constant_dynamic-update-slice_fusion.54
  30.9 0.6 constant_dynamic-update-slice_fusion.34
  35.1 0.6 constant_dynamic-update-slice_fusion.27
  36.4 0.6 constant_dynamic-update-slice_fusion.25
  40.0 0.6 constant_dynamic-update-slice_fusion.19
  51.5 18.8 %all-to-all-start = ((bf16[64,1,1,128,128]{3,4,2,1,0:T(8,128)(2,1)}), bf16[64,1,1,128,128]{3,4,2,1,0:T(8,128)(2,1)S(1)}, u32[]{:S(2)}, u32[]{:S(2)}) async-start(bf16[64,1,1,128,128]{3,4,2,1,0:T(8,128)(2,1)} %constant_dynamic-update-slice_fusion.1), calls=%async_computation | async-start | bytes 4194304 | tf_op jit(solution)/shard_map/all_to_all | solution.py:63
  71.1 99.2 %all-to-all-done = bf16[64,1,1,128,128]{3,4,2,1,0:T(8,128)(2,1)S(1)} async-done(((bf16[64,1,1,128,128]{3,4,2,1,0:T(8,128)(2,1)}), bf16[64,1,1,128,128]{3,4,2,1,0:T(8,128)(2,1)S(1)}, u32[]{:S(2)}, u32[]{:S(2)}) %all-to-all-start) | async-done | bytes 2097184 | tf_op jit(solution)/shard_map/all_to_all | solution.py:63
  170.4 8.0 gather_fusion.1
  178.4 8.7 copy.33
  187.0 6.1 select_bitcast_fusion
  193.1 6.1 all-to-all-start.2
  199.6 7.9 gather_fusion
  207.6 6.0 broadcast_select_fusion
  213.6 265.0 %all-to-all-done.2 = bf16[64,3,1,128,128]{4,3,1,2,0:T(8,128)(2,1)} async-done(((bf16[64,3,1,128,128]{4,3,1,2,0:T(8,128)(2,1)}), bf16[64,3,1,128,128]{4,3,1,2,0:T(8,128)(2,1)}, u32[]{:S(2)}, u32[]{:S(2)}) %all-to-all-start.2) | async-done | bytes 6291488 | tf_op jit(solution)/shard_map/all_to_all | solution.py:86
  478.6 6.1 all-to-all-start.1
  485.0 279.1 %all-to-all-done.1 = bf16[64,3,1,128,128]{3,4,2,1,0:T(8,128)(2,1)} async-done(((bf16[64,3,1,128,128]{3,4,2,1,0:T(8,128)(2,1)}), bf16[64,3,1,128,128]{3,4,2,1,0:T(8,128)(2,1)}, u32[]{:S(2)}, u32[]{:S(2)}) %all-to-all-start.1) | async-done | bytes 6291488 | tf_op jit(solution)/shard_map/all_to_all | solution.py:85
  764.0 92.0 %while.13 = (s32[]{:T(128)}, f32[3,128,1024]{2,1,0:T(8,128)}, s32[3]{0:T(128)S(1)}, bf16[64,3,1,128,128]{3,4,2,1,0:T(8,128)(2,1)}, bf16[64,3,1,128,128]{4,3,1,2,...) while((s32[]{:T(128)}, f32[3,128,1024]{2,1,0:T(8,128)}, ...), condition=%wide.region_6.8_spmd.clone.clone.clone, body=%wide.region_5.7_spmd.clone.clone.clone.sunk | while | flops 2216230912 | bytes 70402800 | solution.py:93
  764.0 0.6 dynamic_slice.27
  766.5 3.2 constant_dynamic-slice_fusion.5
  769.7 3.2 copy.47
  773.7 1.1 fusion.35
  774.8 9.9 %add_convert_fusion.2 = (bf16[8,128,64,1,64]{1,4,3,0,2:T(8,128)(2,1)S(1)}, bf16[8,128,64,1,64]{1,4,3,0,2:T(8,128)(2,1)S(1)}) fusion(f32[8,64,64]{2,0,1:T(8,128)S(1)} %get-tuple-element.222, f32[128,64,64]{0,2,1:T(8,128)S(1)} %get-tuple-element.223, f32[8,64,64]{2,0,1:T(8,128)S(1)} %get-tuple-element.224, f32[128,64,64]{0,2,1:T(8,128)S(1)} %get-tuple-element.225), kind=kLoop, calls=%fused_computation.9.clone.1 | loop fusion | flops 33554432 | bytes 21233664 | tf_op jit(solution)/shard_map/convert.2
  784.8 1.7 constant_dynamic-slice_fusion.4
  786.5 7.1 fusion.36
  793.9 0.8 constant_dynamic-update-slice_fusion.66
  794.7 0.6 dynamic_slice.27
  797.1 3.2 constant_dynamic-slice_fusion.5
  800.4 3.2 copy.47
  804.4 1.1 fusion.35
  805.5 9.9 %add_convert_fusion.2 = (bf16[8,128,64,1,64]{1,4,3,0,2:T(8,128)(2,1)S(1)}, bf16[8,128,64,1,64]{1,4,3,0,2:T(8,128)(2,1)S(1)}) fusion(f32[8,64,64]{2,0,1:T(8,128)S(1)} %get-tuple-element.222, f32[128,64,64]{0,2,1:T(8,128)S(1)} %get-tuple-element.223, f32[8,64,64]{2,0,1:T(8,128)S(1)} %get-tuple-element.224, f32[128,64,64]{0,2,1:T(8,128)S(1)} %get-tuple-element.225), kind=kLoop, calls=%fused_computation.9.clone.1 | loop fusion | flops 33554432 | bytes 21233664 | tf_op jit(solution)/shard_map/convert.2
  815.4 1.7 constant_dynamic-slice_fusion.4
  817.2 7.1 fusion.36
  824.5 0.9 constant_dynamic-update-slice_fusion.66
  825.4 0.6 dynamic_slice.27
  827.8 3.2 constant_dynamic-slice_fusion.5
  831.1 3.2 copy.47
  835.1 1.1 fusion.35
  836.2 9.9 %add_convert_fusion.2 = (bf16[8,128,64,1,64]{1,4,3,0,2:T(8,128)(2,1)S(1)}, bf16[8,128,64,1,64]{1,4,3,0,2:T(8,128)(2,1)S(1)}) fusion(f32[8,64,64]{2,0,1:T(8,128)S(1)} %get-tuple-element.222, f32[128,64,64]{0,2,1:T(8,128)S(1)} %get-tuple-element.223, f32[8,64,64]{2,0,1:T(8,128)S(1)} %get-tuple-element.224, f32[128,64,64]{0,2,1:T(8,128)S(1)} %get-tuple-element.225), kind=kLoop, calls=%fused_computation.9.clone.1 | loop fusion | flops 33554432 | bytes 21233664 | tf_op jit(solution)/shard_map/convert.2
  846.1 1.7 constant_dynamic-slice_fusion.4
  847.9 7.1 fusion.36
  855.3 0.8 constant_dynamic-update-slice_fusion.66
  856.1 2.9 broadcast_multiply_fusion
  859.0 32.6 %reduce-scatter.2.cloned.1.call-done = f32[3,16,1024]{2,1,0:T(8,128)} async-done(((f32[3,128,1024]{2,1,0:T(8,128)}), f32[3,16,1024]{2,1,0:T(8,128)}) %reduce-scatter.2.cloned.1.call-update) | async-done | bytes 196624 | tf_op jit(solution)/shard_map/reduce_scatter | solution.py:95
  (112 shorter events, 40.6 us)
Async XLA Ops:
  10.2 0.7 copy-start.3
  51.5 18.8 %copy-start.2 = (s32[96,3]{0,1:T(4,128)S(1)}, s32[96,3]{0,1:T(4,128)}, u32[]{:S(2)}) copy-start(s32[96,3]{0,1:T(4,128)} %param.9) | copy-start | bytes 3460
  51.5 118.9 %all-to-all-start = ((bf16[64,1,1,128,128]{3,4,2,1,0:T(8,128)(2,1)}), bf16[64,1,1,128,128]{3,4,2,1,0:T(8,128)(2,1)S(1)}, u32[]{:S(2)}, u32[]{:S(2)}) async-start(bf16[64,1,1,128,128]{3,4,2,1,0:T(8,128)(2,1)} %constant_dynamic-update-slice_fusion.1), calls=%async_computation | async-start | bytes 4194304 | tf_op jit(solution)/shard_map/all_to_all | solution.py:63
  193.1 285.5 %all-to-all-start.2 = ((bf16[64,3,1,128,128]{4,3,1,2,0:T(8,128)(2,1)}), bf16[64,3,1,128,128]{4,3,1,2,0:T(8,128)(2,1)}, u32[]{:S(2)}, u32[]{:S(2)}) async-start(bf16[64,3,1,128,128]{4,3,1,2,0:T(8,128)(2,1)} %select_bitcast_fusion), calls=%async_computation.2 | async-start | bytes 12582912 | tf_op jit(solution)/shard_map/all_to_all | solution.py:86
  478.6 285.4 %all-to-all-start.1 = ((bf16[64,3,1,128,128]{3,4,2,1,0:T(8,128)(2,1)}), bf16[64,3,1,128,128]{3,4,2,1,0:T(8,128)(2,1)}, u32[]{:S(2)}, u32[]{:S(2)}) async-start(bf16[64,3,1,128,128]{3,4,2,1,0:T(8,128)(2,1)} %broadcast_select_fusion), calls=%async_computation.1 | async-start | bytes 12582912 | tf_op jit(solution)/shard_map/all_to_all | solution.py:85
  484.7 406.9 %reduce-scatter.2.cloned.1.call-start = ((), (), s32[]{:S(2)}) async-start(), calls=%async_computation.4 | async-start | bytes 1769472 | tf_op jit(solution)/shard_map/reduce_scatter | solution.py:95
  764.0 9.7 %copy-start = (s32[64,64]{1,0:T(8,128)}, s32[64,64]{1,0:T(8,128)S(1)}, u32[]{:S(2)}) copy-start(s32[64,64]{1,0:T(8,128)S(1)} %get-tuple-element.253) | copy-start | bytes 49156 | tf_op jit(solution)/shard_map/while
  793.7 1.0 copy-start.1
  794.7 9.7 %copy-start = (s32[64,64]{1,0:T(8,128)}, s32[64,64]{1,0:T(8,128)S(1)}, u32[]{:S(2)}) copy-start(s32[64,64]{1,0:T(8,128)S(1)} %get-tuple-element.253) | copy-start | bytes 49156 | tf_op jit(solution)/shard_map/while
  824.3 1.1 copy-start.1
  825.4 9.7 %copy-start = (s32[64,64]{1,0:T(8,128)}, s32[64,64]{1,0:T(8,128)S(1)}, u32[]{:S(2)}) copy-start(s32[64,64]{1,0:T(8,128)S(1)} %get-tuple-element.253) | copy-start | bytes 49156 | tf_op jit(solution)/shard_map/while
  855.0 1.0 copy-start.1
Sparse Core Ops, SparseCore 0:
  859.1 32.4 reduce-scatter.1
